TPU v7x, 256 devices: a whole 4x4x8 slice. The times are simulated.
256 devices in a mesh: section: 8 (over x, y_hi), shard: 32 (over z, y_lo, core).
Axes of the slice: x: 4, y: 4 (y_hi: 2, y_lo: 2; y = y_hi * 2 + y_lo), z: 8, core: 2. Of those that a mesh axis runs over, the one named last changes fastest.
Arguments:
- rows: bfloat16 [8, 2048, 6144], P('section', 'shard'), may hold values from -6 to 6
- expert_ids: int32 [8, 2048, 2], P('section', 'shard'), may hold values from 0 to 7, all different within a row; in each aligned block of 64 rows (0 to 63, 64 to 127, ..., all dimensions but the last counted through in order) at most 18 rows name the same one
- gate_probs: float32 [8, 2048, 2], P('section', 'shard'), may hold values from 0.1 to 1
- w_gate: bfloat16 [8, 6144, 8192], P('section', None, 'shard'), may hold values from -0.078125 to 0.078125
- w_up: bfloat16 [8, 6144, 8192], P('section', None, 'shard'), may hold values from -0.078125 to 0.078125
- w_down: bfloat16 [8, 8192, 6144], P('section', 'shard'), may hold values from -0.0625 to 0.0625
Outputs:
- handed: bfloat16 [8, 2048, 6144], P('section', 'shard')
Inputs may be any that keep to these rules, and one draw needn't show every extreme that they name: `expert_ids`: within each section's block of 64 tokens of one shard index, no expert is named by more than 18 tokens, and each token names 2 different experts.
All inputs are finite; a program needn't handle non-finite values.
Results may differ from a plain program's by a relative error of at most 0.011.
Values may be sent and summed in bfloat16 or wider, within the bound.
A program may use at most 128 MiB of HBM per device.

v0:
```python
import jax
import jax.numpy as jnp
from jax import lax
from jax.sharding import PartitionSpec as P

CAP = 18


def from_behind(value, axis, steps):
    count = lax.axis_size(axis)
    pairs = [(source, (source + steps) % count) for source in range(count)]
    return lax.ppermute(value, axis, pairs)


def unpack_rows(slot_values, expert_out, capacity):
    marks = jnp.arange(capacity, dtype=jnp.float32)[:, None]
    placed = (slot_values[None, :] == marks).astype(jnp.bfloat16)
    return lax.dot_general(
        placed, expert_out, (((0,), (0,)), ((), ())), preferred_element_type=jnp.float32
    )


def on_device(rows, expert_ids, gate_probs, w_gate, w_up, w_down):
    tokens = rows[0]
    chosen_ids = expert_ids[0]
    probs = gate_probs[0]
    gate_w = w_gate[0]
    up_w = w_up[0]
    down_w = w_down[0]
    section_num = lax.axis_index("section")
    hit = chosen_ids == section_num
    routed = jnp.any(hit, axis=-1)
    weight = jnp.sum(jnp.where(hit, probs, jnp.float32(0.0)), axis=-1)
    slot = jnp.cumsum(routed.astype(jnp.int32)) - 1
    slot_values = jnp.where(routed, slot, -1).astype(jnp.float32)
    marks = jnp.arange(CAP, dtype=jnp.float32)[:, None]
    placed = (slot_values[None, :] == marks).astype(jnp.bfloat16)
    packed = jnp.dot(placed, tokens, preferred_element_type=jnp.float32).astype(jnp.bfloat16)
    piece = lax.all_gather(packed, "shard", axis=0, tiled=True)
    gate = jnp.dot(piece, gate_w, preferred_element_type=jnp.float32)
    upper = jnp.dot(piece, up_w, preferred_element_type=jnp.float32)
    hidden_all = (jax.nn.silu(gate) * upper).astype(jnp.bfloat16)
    expert_out = lax.psum_scatter(
        jnp.dot(hidden_all, down_w, preferred_element_type=jnp.float32).astype(jnp.bfloat16),
        "shard",
        scatter_dimension=0,
        tiled=True,
    )
    per_token = unpack_rows(slot_values, expert_out, CAP)
    layer_out = (tokens.astype(jnp.float32) + weight[:, None] * per_token).astype(jnp.bfloat16)
    handed = from_behind(layer_out, "section", 1)
    return handed[None]


def solution(mesh):
    in_specs = (
        P("section", "shard", None),
        P("section", "shard", None),
        P("section", "shard", None),
        P("section", None, "shard"),
        P("section", None, "shard"),
        P("section", "shard", None),
    )
    out_specs = P("section", "shard", None)
    return jax.shard_map(
        on_device, mesh=mesh, in_specs=in_specs, out_specs=out_specs, check_vma=False
    )
```

profile of v0, /device:TPU:40, one launch (start us, length us, event | category | flops | bytes accessed | tf_op | source)
XLA Modules:
  0.0 356.0 jit_solution(13705711673027606384)
XLA Ops:
  7.7 2.1 fusion.3
  9.8 75.4 %all-gather.3.cloned.1.call-done = bf16[32,18,6144]{2,1,0:T(8,128)(2,1)} async-done(((bf16[1,18,6144]{2,1,0:T(8,128)(2,1)}), bf16[32,18,6144]{2,1,0:T(8,128)(2,1)}) %all-gather.3.cloned.1.call-update) | async-done | bytes 7077904 | tf_op jit(solution)/shard_map/all_gather | solution.py:39
  85.3 9.6 %reshape.43 = bf16[576,6144]{1,0:T(8,128)(2,1)} reshape(bf16[32,18,6144]{2,1,0:T(8,128)(2,1)} %all-gather.3.cloned.1.call-done) | data formatting | bytes 14155776
  94.9 6.0 %fusion.7 = f32[576,256]{1,0:T(8,128)S(1)} fusion(bf16[576,6144]{1,0:T(8,128)(2,1)} %reshape.43, bf16[1,6144,256]{2,1,0:T(8,128)(2,1)} %param.9), kind=kOutput, calls=%fused_computation.9 | convolution fusion | flops 1811939328 | bytes 10813440 | tf_op jit(solution)/shard_map/dot_general | solution.py:40
  101.7 2.0 fusion.12
  103.7 4.9 %convolution_convert_fusion = bf16[576,6144]{1,0:T(8,128)(2,1)} fusion(bf16[576,256]{1,0:T(8,128)(2,1)S(1)} %fusion.12, bf16[1,256,6144]{2,1,0:T(8,128)(2,1)S(1)} %copy-done), kind=kOutput, calls=%fused_computation | convolution fusion | flops 1815478272 | bytes 10518528 | tf_op jit(solution)/shard_map/dot_general | solution.py:44
  108.6 108.9 %fusion = bf16[24,6144]{1,0:T(8,128)(2,1)S(1)} fusion(bf16[576,6144]{1,0:T(8,128)(2,1)} %convolution_convert_fusion), kind=kCustom, calls=%all-reduce-scatter | all-reduce-scatter fusion | flops 4718593 | bytes 7373824
  217.5 1.9 collective-permute-start.1
  219.4 1.9 collective-permute-start.2
  221.4 3.0 collective-permute-start.8
  224.5 3.5 collective-permute-start.3
  228.0 3.1 collective-permute-start.4
  231.1 10.0 %collective-permute-done.8 = bf16[18,6144]{1,0:T(8,128)(2,1)S(1)} collective-permute-done((bf16[18,6144]{1,0:T(8,128)(2,1)S(1)}, bf16[18,6144]{1,0:T(8,128)(2,1)S(1)}, u32[]{:S(2)}, u32[]{:S(2)}) %collective-permute-start.8) | collective-permute-done | bytes 221216
  241.1 3.7 %collective-permute-start.5 = (bf16[24,6144]{1,0:T(8,128)(2,1)S(1)}, bf16[24,6144]{1,0:T(8,128)(2,1)}, u32[]{:S(2)}, u32[]{:S(2)}) collective-permute-start(bf16[24,6144]{1,0:T(8,128)(2,1)S(1)} %fusion), channel_id=1, source_target_pairs={{0,5},{1,6},{2,7},{3,8},{4,9},{5,10},{6,11},{7,12},{8,13},{9,14},{... | collective-permute-start | bytes 884744
  244.8 1.9 collective-permute-start.6
  246.8 7.8 %collective-permute-start.7 = (bf16[24,6144]{1,0:T(8,128)(2,1)S(1)}, bf16[24,6144]{1,0:T(8,128)(2,1)}, u32[]{:S(2)}, u32[]{:S(2)}) collective-permute-start(bf16[24,6144]{1,0:T(8,128)(2,1)S(1)} %fusion), channel_id=1, source_target_pairs={{0,7},{1,8},{2,9},{3,10},{4,11},{5,12},{6,13},{7,14},{8,15},{9,16}... | collective-permute-start | bytes 884744
  256.0 13.5 %collective-permute-done.4 = bf16[24,6144]{1,0:T(8,128)(2,1)} collective-permute-done((bf16[24,6144]{1,0:T(8,128)(2,1)S(1)}, bf16[24,6144]{1,0:T(8,128)(2,1)}, u32[]{:S(2)}, u32[]{:S(2)}) %collective-permute-start.4) | collective-permute-done | bytes 294944
  269.5 6.3 %collective-permute-done.5 = bf16[24,6144]{1,0:T(8,128)(2,1)} collective-permute-done((bf16[24,6144]{1,0:T(8,128)(2,1)S(1)}, bf16[24,6144]{1,0:T(8,128)(2,1)}, u32[]{:S(2)}, u32[]{:S(2)}) %collective-permute-start.5) | collective-permute-done | bytes 294944
  275.9 6.3 %collective-permute-done.6 = bf16[24,6144]{1,0:T(8,128)(2,1)} collective-permute-done((bf16[24,6144]{1,0:T(8,128)(2,1)S(1)}, bf16[24,6144]{1,0:T(8,128)(2,1)}, u32[]{:S(2)}, u32[]{:S(2)}) %collective-permute-start.6) | collective-permute-done | bytes 294944
  282.2 6.3 %collective-permute-done.7 = bf16[24,6144]{1,0:T(8,128)(2,1)} collective-permute-done((bf16[24,6144]{1,0:T(8,128)(2,1)S(1)}, bf16[24,6144]{1,0:T(8,128)(2,1)}, u32[]{:S(2)}, u32[]{:S(2)}) %collective-permute-start.7) | collective-permute-done | bytes 294944
  288.5 34.5 %concatenate = bf16[210,6144]{1,0:T(8,128)(2,1)} concatenate(bf16[18,6144]{1,0:T(8,128)(2,1)} %copy-done.4, bf16[24,6144]{1,0:T(8,128)(2,1)} %collective-permute-done.7, bf16[24,6144]{1,0:T(8,128)(2,1)} %collective-permute-done.6, bf16[24,6144]{1,0:T(8,128)(2,1)} %collective-permute-done.5, bf16[24,6144]{1,0:T(8,128)(2,1)} %collective-permute-done.4, ...), dimensions={0} | concatenate | bytes 5160960
  323.0 1.7 fusion.2
  324.7 2.2 collective-permute-start
  326.9 21.4 %collective-permute-done = bf16[64,6144]{1,0:T(8,128)(2,1)S(1)} collective-permute-done((bf16[64,6144]{1,0:T(8,128)(2,1)S(1)}, bf16[64,6144]{1,0:T(8,128)(2,1)S(1)}, u32[]{:S(2)}, u32[]{:S(2)}) %collective-permute-start) | collective-permute-done | bytes 786464 | tf_op jit(solution)/shard_map/ppermute | solution.py:12
  (33 shorter events, 3.6 us)
Async XLA Ops:
  6.5 97.1 %copy-start = (bf16[1,256,6144]{2,1,0:T(8,128)(2,1)S(1)}, bf16[1,256,6144]{2,1,0:T(8,128)(2,1)}, u32[]{:S(2)}) copy-start(bf16[1,256,6144]{2,1,0:T(8,128)(2,1)} %param.11) | copy-start | bytes 9437188
  6.5 78.7 %all-gather.3.cloned.1.call-start = ((), (), s32[]{:S(2)}) async-start(), calls=%async_computation | async-start | bytes 9732096 | tf_op jit(solution)/shard_map/all_gather | solution.py:39
  94.8 6.1 %copy-start.1 = (bf16[576,6144]{1,0:T(8,128)(2,1)S(1)}, bf16[576,6144]{1,0:T(8,128)(2,1)}, u32[]{:S(2)}) copy-start(bf16[576,6144]{1,0:T(8,128)(2,1)} %reshape.43) | copy-start | bytes 21233668
  94.8 6.8 %copy-start.8 = (bf16[1,6144,256]{2,1,0:T(8,128)(2,1)S(1)}, bf16[1,6144,256]{2,1,0:T(8,128)(2,1)}, u32[]{:S(2)}) copy-start(bf16[1,6144,256]{2,1,0:T(8,128)(2,1)} %param.10) | copy-start | bytes 9437188
  108.6 146.0 %copy-start.7 = (u32[256]{0:T(256)S(1)}, u32[256]{0:T(256)}, u32[]{:S(2)}) copy-start(u32[256]{0:T(256)} %constant.29) | copy-start | bytes 3076
  108.6 147.4 %copy-start.5 = (s32[1,64,2]{1,2,0:T(2,128)S(1)}, s32[1,64,2]{1,2,0:T(2,128)}, u32[]{:S(2)}) copy-start(s32[1,64,2]{1,2,0:T(2,128)} %param.7) | copy-start | bytes 1540
  108.6 147.4 %copy-start.6 = (f32[1,64,2]{1,2,0:T(2,128)S(1)}, f32[1,64,2]{1,2,0:T(2,128)}, u32[]{:S(2)}) copy-start(f32[1,64,2]{1,2,0:T(2,128)} %param.8) | copy-start | bytes 1540
  217.5 27.3 %collective-permute-start.1 = (bf16[24,6144]{1,0:T(8,128)(2,1)S(1)}, bf16[24,6144]{1,0:T(8,128)(2,1)S(1)}, u32[]{:S(2)}, u32[]{:S(2)}) collective-permute-start(bf16[24,6144]{1,0:T(8,128)(2,1)S(1)} %fusion), channel_id=1, source_target_pairs={{0,1},{1,2},{2,3},{3,4},{4,5},{5,6},{6,7},{7,8},{8,9},{9,10},{10,1... | collective-permute-start | bytes 884744
  219.4 27.3 %collective-permute-start.2 = (bf16[24,6144]{1,0:T(8,128)(2,1)S(1)}, bf16[24,6144]{1,0:T(8,128)(2,1)S(1)}, u32[]{:S(2)}, u32[]{:S(2)}) collective-permute-start(bf16[24,6144]{1,0:T(8,128)(2,1)S(1)} %fusion), channel_id=1, source_target_pairs={{0,2},{1,3},{2,4},{3,5},{4,6},{5,7},{6,8},{7,9},{8,10},{9,11},{10,... | collective-permute-start | bytes 884744
  221.4 19.7 %collective-permute-start.8 = (bf16[18,6144]{1,0:T(8,128)(2,1)S(1)}, bf16[18,6144]{1,0:T(8,128)(2,1)S(1)}, u32[]{:S(2)}, u32[]{:S(2)}) collective-permute-start(bf16[18,6144]{1,0:T(8,128)(2,1)S(1)} %slice), channel_id=1, source_target_pairs={{0,8},{1,9},{2,10},{3,11},{4,12},{5,13},{6,14},{7,15},{8,16},{9,17... | collective-permute-start | bytes 663560
  224.5 31.5 %collective-permute-start.3 = (bf16[24,6144]{1,0:T(8,128)(2,1)S(1)}, bf16[24,6144]{1,0:T(8,128)(2,1)}, u32[]{:S(2)}, u32[]{:S(2)}) collective-permute-start(bf16[24,6144]{1,0:T(8,128)(2,1)S(1)} %fusion), channel_id=1, source_target_pairs={{0,3},{1,4},{2,5},{3,6},{4,7},{5,8},{6,9},{7,10},{8,11},{9,12},{10... | collective-permute-start | bytes 884744
  228.0 41.5 %collective-permute-start.4 = (bf16[24,6144]{1,0:T(8,128)(2,1)S(1)}, bf16[24,6144]{1,0:T(8,128)(2,1)}, u32[]{:S(2)}, u32[]{:S(2)}) collective-permute-start(bf16[24,6144]{1,0:T(8,128)(2,1)S(1)} %fusion), channel_id=1, source_target_pairs={{0,4},{1,5},{2,6},{3,7},{4,8},{5,9},{6,10},{7,11},{8,12},{9,13},{1... | collective-permute-start | bytes 884744
  241.1 13.5 %copy-start.4 = (bf16[18,6144]{1,0:T(8,128)(2,1)}, bf16[18,6144]{1,0:T(8,128)(2,1)S(1)}, u32[]{:S(2)}) copy-start(bf16[18,6144]{1,0:T(8,128)(2,1)S(1)} %collective-permute-done.8) | copy-start | bytes 663556
  241.1 34.8 %collective-permute-start.5 = (bf16[24,6144]{1,0:T(8,128)(2,1)S(1)}, bf16[24,6144]{1,0:T(8,128)(2,1)}, u32[]{:S(2)}, u32[]{:S(2)}) collective-permute-start(bf16[24,6144]{1,0:T(8,128)(2,1)S(1)} %fusion), channel_id=1, source_target_pairs={{0,5},{1,6},{2,7},{3,8},{4,9},{5,10},{6,11},{7,12},{8,13},{9,14},{... | collective-permute-start | bytes 884744
  244.8 2.0 copy-start.2
  244.8 37.4 %collective-permute-start.6 = (bf16[24,6144]{1,0:T(8,128)(2,1)S(1)}, bf16[24,6144]{1,0:T(8,128)(2,1)}, u32[]{:S(2)}, u32[]{:S(2)}) collective-permute-start(bf16[24,6144]{1,0:T(8,128)(2,1)S(1)} %fusion), channel_id=1, source_target_pairs={{0,6},{1,7},{2,8},{3,9},{4,10},{5,11},{6,12},{7,13},{8,14},{9,15},... | collective-permute-start | bytes 884744
  246.7 7.8 %copy-start.3 = (bf16[24,6144]{1,0:T(8,128)(2,1)}, bf16[24,6144]{1,0:T(8,128)(2,1)S(1)}, u32[]{:S(2)}) copy-start(bf16[24,6144]{1,0:T(8,128)(2,1)S(1)} %collective-permute-done.2) | copy-start | bytes 884740
  246.8 41.7 %collective-permute-start.7 = (bf16[24,6144]{1,0:T(8,128)(2,1)S(1)}, bf16[24,6144]{1,0:T(8,128)(2,1)}, u32[]{:S(2)}, u32[]{:S(2)}) collective-permute-start(bf16[24,6144]{1,0:T(8,128)(2,1)S(1)} %fusion), channel_id=1, source_target_pairs={{0,7},{1,8},{2,9},{3,10},{4,11},{5,12},{6,13},{7,14},{8,15},{9,16}... | collective-permute-start | bytes 884744
  324.7 23.6 %collective-permute-start = (bf16[64,6144]{1,0:T(8,128)(2,1)S(1)}, bf16[64,6144]{1,0:T(8,128)(2,1)S(1)}, u32[]{:S(2)}, u32[]{:S(2)}) collective-permute-start(bf16[64,6144]{1,0:T(8,128)(2,1)S(1)} %fusion.2), channel_id=1, source_target_pairs={{0,32},{32,64},{64,96},{96,128},{128,160},{160,192},{192,224},{224... | collective-permute-start | bytes 2359304 | tf_op jit(solution)/shard_map/ppermute | solution.py:12
Sparse Core Ops, SparseCore 0:
  9.9 75.2 all-gather.2
where the time goes:
time: 359 us; the launch traced here: 356 us
  waiting for transfers between devices  139 us (39%)
  blocking collectives  109 us (30%)
  local copies, waits for them, and re-layouts  46.6 us (13%)
  starting transfers between devices  29.1 us (8%)
  matrix products  16.7 us (5%)
  between operations  14.3 us (4%)
    unnamed x1, blocking collectives  109 us
    all_gather x1, waiting for transfers between devices, on_device(): piece = lax.all_gather(packed, 'shard', axis=0, tiled=True)  75.4 us
    unnamed x23, local copies, waits for them, and re-layouts  46.5 us
    unnamed x9, waiting for transfers between devices  42.5 us
    unnamed x8, starting transfers between devices  26.9 us
    ppermute x1, waiting for transfers between devices, from_behind(): return lax.ppermute(value, axis, pairs)  21.4 us
  transfers between devices with their start and end apart: 10, of which 7 were waited for; matrix products, arithmetic and copies ran while one was open for 0% of the time, Pallas kernels for 0%

commit v1 on v0

--- a/solution.py
+++ b/solution.py
@@ -36,7 +36,9 @@
     marks = jnp.arange(CAP, dtype=jnp.float32)[:, None]
     placed = (slot_values[None, :] == marks).astype(jnp.bfloat16)
     packed = jnp.dot(placed, tokens, preferred_element_type=jnp.float32).astype(jnp.bfloat16)
-    piece = lax.all_gather(packed, "shard", axis=0, tiled=True)
+    piece = jnp.concatenate(
+        lax.all_to_all(jnp.stack([packed] * lax.axis_size("shard")), "shard", 0, 0), axis=0
+    )
     gate = jnp.dot(piece, gate_w, preferred_element_type=jnp.float32)
     upper = jnp.dot(piece, up_w, preferred_element_type=jnp.float32)
     hidden_all = (jax.nn.silu(gate) * upper).astype(jnp.bfloat16)

time: 359 us -> 487 us (1.36)
  blocking collectives: 109 us -> 326 us
  waiting for transfers between devices: 139 us -> 64 us
  between operations: 14.3 us -> 0.83 us
    all_to_all x0 -> x1, blocking collectives: none -> 217 us  [on_device(): lax.all_to_all(jnp.stack([packed] * lax.axis_size('shard')), 'shard', 0, 0)]
    all_gather x1 -> x0, waiting for transfers between devices: 75.4 us -> none  [on_device(): piece = lax.all_gather(packed, 'shard', axis=0, tiled=True)]
    unnamed x23 -> x22, local copies, waits for them, and re-layouts: 46.5 us -> 36.7 us
    reshape x0 -> x1, local copies, waits for them, and re-layouts: none -> 9.61 us  [on_device(): jnp.concatenate(lax.all_to_all(jnp.stack([packed] * lax.axis_size('shard'...]
    unnamed x9 -> x8, waiting for transfers between devices: 42.5 us -> 42.4 us
  transfers between devices with their start and end apart: 10 -> 9, of which waited for: 7 -> 6; matrix products, arithmetic and copies ran while one was open for 0% -> 0% of each run, Pallas kernels for 0% -> 0%
where the time goes in v1:
time: 487 us; the launch traced here: 484 us
  blocking collectives  326 us (67%)
  waiting for transfers between devices  64 us (13%)
  local copies, waits for them, and re-layouts  47.5 us (10%)
  starting transfers between devices  28.9 us (6%)
  matrix products  16 us (3%)
    all_to_all x1, blocking collectives, on_device(): lax.all_to_all(jnp.stack([packed] * lax.axis_size('shard')), 'shard', 0, 0)  217 us
    unnamed x1, blocking collectives  108 us
    unnamed x8, waiting for transfers between devices  42.4 us
    unnamed x22, local copies, waits for them, and re-layouts  36.7 us
    unnamed x8, starting transfers between devices  26.5 us
    ppermute x1, waiting for transfers between devices, from_behind(): return lax.ppermute(value, axis, pairs)  21.7 us
  transfers between devices with their start and end apart: 9, of which 6 were waited for; matrix products, arithmetic and copies ran while one was open for 0% of the time, Pallas kernels for 0%

profile of v1, /device:TPU:40, one launch (start us, length us, event | category | flops | bytes accessed | tf_op | source)
XLA Modules:
  0.0 484.0 jit_solution(10935402019314050768)
XLA Ops:
  1.2 1.4 convolution_convert_fusion.1
  3.7 217.4 %all_to_all.5 = bf16[32,18,6144]{2,1,0:T(8,128)(2,1)} all-to-all(bf16[32,18,6144]{2,1,0:T(8,128)(2,1)S(1)} %stack.2), channel_id=1, replica_groups=mesh['section'=8,'shard'=32] {'shard'}, dimensions={0} | all-to-all | bytes 14155776 | tf_op jit(solution)/shard_map/all_to_all | solution.py:40
  221.1 9.6 %reshape.46 = bf16[576,6144]{1,0:T(8,128)(2,1)} reshape(bf16[32,18,6144]{2,1,0:T(8,128)(2,1)} %all_to_all.5) | data formatting | bytes 14155776 | tf_op jit(solution)/shard_map/reshape | solution.py:39
  230.7 6.0 %fusion.6 = f32[576,256]{1,0:T(8,128)S(1)} fusion(bf16[576,6144]{1,0:T(8,128)(2,1)} %reshape.46, bf16[1,6144,256]{2,1,0:T(8,128)(2,1)} %param.9), kind=kOutput, calls=%fused_computation.8 | convolution fusion | flops 1811939328 | bytes 10813440 | tf_op jit(solution)/shard_map/dot_general | solution.py:42
  237.5 2.0 fusion.11
  239.5 4.9 %convolution_convert_fusion = bf16[576,6144]{1,0:T(8,128)(2,1)} fusion(bf16[576,256]{1,0:T(8,128)(2,1)S(1)} %fusion.11, bf16[1,256,6144]{2,1,0:T(8,128)(2,1)S(1)} %copy-done), kind=kOutput, calls=%fused_computation | convolution fusion | flops 1815478272 | bytes 10518528 | tf_op jit(solution)/shard_map/dot_general | solution.py:46
  244.4 108.2 %fusion = bf16[24,6144]{1,0:T(8,128)(2,1)S(1)} fusion(bf16[576,6144]{1,0:T(8,128)(2,1)} %convolution_convert_fusion), kind=kCustom, calls=%all-reduce-scatter | all-reduce-scatter fusion | flops 4718593 | bytes 7373824
  352.7 1.9 collective-permute-start.1
  354.6 1.9 collective-permute-start.2
  356.6 3.0 collective-permute-start.8
  359.6 2.3 collective-permute-start.3
  362.0 3.2 collective-permute-start.4
  365.2 10.5 %collective-permute-done.8 = bf16[18,6144]{1,0:T(8,128)(2,1)S(1)} collective-permute-done((bf16[18,6144]{1,0:T(8,128)(2,1)S(1)}, bf16[18,6144]{1,0:T(8,128)(2,1)S(1)}, u32[]{:S(2)}, u32[]{:S(2)}) %collective-permute-start.8) | collective-permute-done | bytes 221216
  375.7 4.2 collective-permute-start.5
  379.9 1.9 collective-permute-start.6
  381.8 8.0 %collective-permute-start.7 = (bf16[24,6144]{1,0:T(8,128)(2,1)S(1)}, bf16[24,6144]{1,0:T(8,128)(2,1)}, u32[]{:S(2)}, u32[]{:S(2)}) collective-permute-start(bf16[24,6144]{1,0:T(8,128)(2,1)S(1)} %fusion), channel_id=1, source_target_pairs={{0,7},{1,8},{2,9},{3,10},{4,11},{5,12},{6,13},{7,14},{8,15},{9,16}... | collective-permute-start | bytes 884744
  391.2 12.9 %collective-permute-done.4 = bf16[24,6144]{1,0:T(8,128)(2,1)} collective-permute-done((bf16[24,6144]{1,0:T(8,128)(2,1)S(1)}, bf16[24,6144]{1,0:T(8,128)(2,1)}, u32[]{:S(2)}, u32[]{:S(2)}) %collective-permute-start.4) | collective-permute-done | bytes 294944
  404.1 6.3 %collective-permute-done.5 = bf16[24,6144]{1,0:T(8,128)(2,1)} collective-permute-done((bf16[24,6144]{1,0:T(8,128)(2,1)S(1)}, bf16[24,6144]{1,0:T(8,128)(2,1)}, u32[]{:S(2)}, u32[]{:S(2)}) %collective-permute-start.5) | collective-permute-done | bytes 294944
  410.4 6.3 %collective-permute-done.6 = bf16[24,6144]{1,0:T(8,128)(2,1)} collective-permute-done((bf16[24,6144]{1,0:T(8,128)(2,1)S(1)}, bf16[24,6144]{1,0:T(8,128)(2,1)}, u32[]{:S(2)}, u32[]{:S(2)}) %collective-permute-start.6) | collective-permute-done | bytes 294944
  416.7 6.3 %collective-permute-done.7 = bf16[24,6144]{1,0:T(8,128)(2,1)} collective-permute-done((bf16[24,6144]{1,0:T(8,128)(2,1)S(1)}, bf16[24,6144]{1,0:T(8,128)(2,1)}, u32[]{:S(2)}, u32[]{:S(2)}) %collective-permute-start.7) | collective-permute-done | bytes 294944
  423.1 34.3 %concatenate = bf16[210,6144]{1,0:T(8,128)(2,1)} concatenate(bf16[18,6144]{1,0:T(8,128)(2,1)} %copy-done.4, bf16[24,6144]{1,0:T(8,128)(2,1)} %collective-permute-done.7, bf16[24,6144]{1,0:T(8,128)(2,1)} %collective-permute-done.6, bf16[24,6144]{1,0:T(8,128)(2,1)} %collective-permute-done.5, bf16[24,6144]{1,0:T(8,128)(2,1)} %collective-permute-done.4, ...), dimensions={0} | concatenate | bytes 5160960
  457.4 1.7 fusion.2
  459.1 2.4 collective-permute-start
  461.4 21.7 %collective-permute-done = bf16[64,6144]{1,0:T(8,128)(2,1)S(1)} collective-permute-done((bf16[64,6144]{1,0:T(8,128)(2,1)S(1)}, bf16[64,6144]{1,0:T(8,128)(2,1)S(1)}, u32[]{:S(2)}, u32[]{:S(2)}) %collective-permute-start) | collective-permute-done | bytes 786464 | tf_op jit(solution)/shard_map/ppermute | solution.py:12
  (32 shorter events, 4.7 us)
Async XLA Ops:
  0.0 239.5 %copy-start = (bf16[1,256,6144]{2,1,0:T(8,128)(2,1)S(1)}, bf16[1,256,6144]{2,1,0:T(8,128)(2,1)}, u32[]{:S(2)}) copy-start(bf16[1,256,6144]{2,1,0:T(8,128)(2,1)} %param.11) | copy-start | bytes 9437188
  230.7 6.1 %copy-start.1 = (bf16[576,6144]{1,0:T(8,128)(2,1)S(1)}, bf16[576,6144]{1,0:T(8,128)(2,1)}, u32[]{:S(2)}) copy-start(bf16[576,6144]{1,0:T(8,128)(2,1)} %reshape.46) | copy-start | bytes 21233668
  230.7 6.8 %copy-start.8 = (bf16[1,6144,256]{2,1,0:T(8,128)(2,1)S(1)}, bf16[1,6144,256]{2,1,0:T(8,128)(2,1)}, u32[]{:S(2)}) copy-start(bf16[1,6144,256]{2,1,0:T(8,128)(2,1)} %param.10) | copy-start | bytes 9437188
  244.4 145.4 %copy-start.7 = (u32[256]{0:T(256)S(1)}, u32[256]{0:T(256)}, u32[]{:S(2)}) copy-start(u32[256]{0:T(256)} %constant.29) | copy-start | bytes 3076
  244.4 146.7 %copy-start.5 = (s32[1,64,2]{1,2,0:T(2,128)S(1)}, s32[1,64,2]{1,2,0:T(2,128)}, u32[]{:S(2)}) copy-start(s32[1,64,2]{1,2,0:T(2,128)} %param.7) | copy-start | bytes 1540
  244.4 146.7 %copy-start.6 = (f32[1,64,2]{1,2,0:T(2,128)S(1)}, f32[1,64,2]{1,2,0:T(2,128)}, u32[]{:S(2)}) copy-start(f32[1,64,2]{1,2,0:T(2,128)} %param.8) | copy-start | bytes 1540
  352.7 27.2 %collective-permute-start.1 = (bf16[24,6144]{1,0:T(8,128)(2,1)S(1)}, bf16[24,6144]{1,0:T(8,128)(2,1)S(1)}, u32[]{:S(2)}, u32[]{:S(2)}) collective-permute-start(bf16[24,6144]{1,0:T(8,128)(2,1)S(1)} %fusion), channel_id=1, source_target_pairs={{0,1},{1,2},{2,3},{3,4},{4,5},{5,6},{6,7},{7,8},{8,9},{9,10},{10,1... | collective-permute-start | bytes 884744
  354.6 27.2 %collective-permute-start.2 = (bf16[24,6144]{1,0:T(8,128)(2,1)S(1)}, bf16[24,6144]{1,0:T(8,128)(2,1)S(1)}, u32[]{:S(2)}, u32[]{:S(2)}) collective-permute-start(bf16[24,6144]{1,0:T(8,128)(2,1)S(1)} %fusion), channel_id=1, source_target_pairs={{0,2},{1,3},{2,4},{3,5},{4,6},{5,7},{6,8},{7,9},{8,10},{9,11},{10,... | collective-permute-start | bytes 884744
  356.6 19.1 %collective-permute-start.8 = (bf16[18,6144]{1,0:T(8,128)(2,1)S(1)}, bf16[18,6144]{1,0:T(8,128)(2,1)S(1)}, u32[]{:S(2)}, u32[]{:S(2)}) collective-permute-start(bf16[18,6144]{1,0:T(8,128)(2,1)S(1)} %slice), channel_id=1, source_target_pairs={{0,8},{1,9},{2,10},{3,11},{4,12},{5,13},{6,14},{7,15},{8,16},{9,17... | collective-permute-start | bytes 663560
  359.6 31.5 %collective-permute-start.3 = (bf16[24,6144]{1,0:T(8,128)(2,1)S(1)}, bf16[24,6144]{1,0:T(8,128)(2,1)}, u32[]{:S(2)}, u32[]{:S(2)}) collective-permute-start(bf16[24,6144]{1,0:T(8,128)(2,1)S(1)} %fusion), channel_id=1, source_target_pairs={{0,3},{1,4},{2,5},{3,6},{4,7},{5,8},{6,9},{7,10},{8,11},{9,12},{10... | collective-permute-start | bytes 884744
  362.0 42.1 %collective-permute-start.4 = (bf16[24,6144]{1,0:T(8,128)(2,1)S(1)}, bf16[24,6144]{1,0:T(8,128)(2,1)}, u32[]{:S(2)}, u32[]{:S(2)}) collective-permute-start(bf16[24,6144]{1,0:T(8,128)(2,1)S(1)} %fusion), channel_id=1, source_target_pairs={{0,4},{1,5},{2,6},{3,7},{4,8},{5,9},{6,10},{7,11},{8,12},{9,13},{1... | collective-permute-start | bytes 884744
  375.7 14.2 %copy-start.4 = (bf16[18,6144]{1,0:T(8,128)(2,1)}, bf16[18,6144]{1,0:T(8,128)(2,1)S(1)}, u32[]{:S(2)}) copy-start(bf16[18,6144]{1,0:T(8,128)(2,1)S(1)} %collective-permute-done.8) | copy-start | bytes 663556
  375.7 34.8 %collective-permute-start.5 = (bf16[24,6144]{1,0:T(8,128)(2,1)S(1)}, bf16[24,6144]{1,0:T(8,128)(2,1)}, u32[]{:S(2)}, u32[]{:S(2)}) collective-permute-start(bf16[24,6144]{1,0:T(8,128)(2,1)S(1)} %fusion), channel_id=1, source_target_pairs={{0,5},{1,6},{2,7},{3,8},{4,9},{5,10},{6,11},{7,12},{8,13},{9,14},{... | collective-permute-start | bytes 884744
  379.9 2.0 copy-start.2
  379.9 36.9 %collective-permute-start.6 = (bf16[24,6144]{1,0:T(8,128)(2,1)S(1)}, bf16[24,6144]{1,0:T(8,128)(2,1)}, u32[]{:S(2)}, u32[]{:S(2)}) collective-permute-start(bf16[24,6144]{1,0:T(8,128)(2,1)S(1)} %fusion), channel_id=1, source_target_pairs={{0,6},{1,7},{2,8},{3,9},{4,10},{5,11},{6,12},{7,13},{8,14},{9,15},... | collective-permute-start | bytes 884744
  381.8 8.1 %copy-start.3 = (bf16[24,6144]{1,0:T(8,128)(2,1)}, bf16[24,6144]{1,0:T(8,128)(2,1)S(1)}, u32[]{:S(2)}) copy-start(bf16[24,6144]{1,0:T(8,128)(2,1)S(1)} %collective-permute-done.2) | copy-start | bytes 884740
  381.8 41.2 %collective-permute-start.7 = (bf16[24,6144]{1,0:T(8,128)(2,1)S(1)}, bf16[24,6144]{1,0:T(8,128)(2,1)}, u32[]{:S(2)}, u32[]{:S(2)}) collective-permute-start(bf16[24,6144]{1,0:T(8,128)(2,1)S(1)} %fusion), channel_id=1, source_target_pairs={{0,7},{1,8},{2,9},{3,10},{4,11},{5,12},{6,13},{7,14},{8,15},{9,16}... | collective-permute-start | bytes 884744
  459.1 24.0 %collective-permute-start = (bf16[64,6144]{1,0:T(8,128)(2,1)S(1)}, bf16[64,6144]{1,0:T(8,128)(2,1)S(1)}, u32[]{:S(2)}, u32[]{:S(2)}) collective-permute-start(bf16[64,6144]{1,0:T(8,128)(2,1)S(1)} %fusion.2), channel_id=1, source_target_pairs={{0,32},{32,64},{64,96},{96,128},{128,160},{160,192},{192,224},{224... | collective-permute-start | bytes 2359304 | tf_op jit(solution)/shard_map/ppermute | solution.py:12
